TPU v7x, 32 devices: a whole 2x2x4 slice. The times are simulated.
32 devices in a mesh: dp: 2 (over y), seq: 4 (over z), tensor: 4 (over x, core).
Axes of the slice: x: 2, y: 2, z: 4, core: 2. Of those that a mesh axis runs over, the one named last changes fastest.
Arguments:
- layer_input: bfloat16 [6, 1024, 2048], P('dp', 'seq'), may hold values from -6 to 6
- lengths: int32 [6], P('dp'), may hold values from 256 to 1024, as said below
- cotangent: bfloat16 [6, 1024, 2048], P('dp', ('seq', 'tensor')), may hold values from -6 to 6
- ln1_gain: bfloat16 [2048], replicated, may hold values from 0.5 to 1.5
- ln1_bias: bfloat16 [2048], replicated, may hold values from -3 to 3
- w_query: bfloat16 [2048, 2048], P(None, 'tensor'), may hold values from -0.125 to 0.125
- b_query: bfloat16 [2048], P('tensor'), may hold values from -3 to 3
- w_kv: bfloat16 [2048, 256], replicated, may hold values from -0.125 to 0.125
- b_value: bfloat16 [128], replicated, may hold values from -3 to 3
- w_out: bfloat16 [2048, 2048], P('tensor'), may hold values from -0.5 to 0.5
- b_out: bfloat16 [2048], replicated, may hold values from -3 to 3
- ln2_gain: bfloat16 [2048], replicated, may hold values from 0.5 to 1.5
- ln2_bias: bfloat16 [2048], replicated, may hold values from -3 to 3
- w_up: bfloat16 [2048, 8192], P(None, 'tensor'), may hold values from -0.125 to 0.125
- b_up: bfloat16 [8192], P('tensor'), may hold values from -3 to 3
- w_down: bfloat16 [8192, 2048], P('tensor'), may hold values from -0.0625 to 0.0625
- b_down: bfloat16 [2048], replicated, may hold values from -3 to 3
Outputs:
- layer_output: bfloat16 [6, 1024, 2048], P('dp', ('seq', 'tensor'))
- input_grad: float32 [6, 1024, 2048], P('dp', ('seq', 'tensor'))
- g_w_query: float32 [2048, 2048], P(('dp', 'seq'), 'tensor')
- g_b_query: float32 [16, 128], P('tensor', ('dp', 'seq'))
- g_w_kv: float32 [2048, 256], P(('dp', 'seq', 'tensor'))
- g_b_value: float32 [128], P(('dp', 'seq', 'tensor'))
- g_w_out: float32 [2048, 2048], P('tensor', ('dp', 'seq'))
- g_w_up: float32 [2048, 8192], P(('dp', 'seq'), 'tensor')
- g_b_up: float32 [64, 128], P('tensor', ('dp', 'seq'))
- g_w_down: float32 [8192, 2048], P('tensor', ('dp', 'seq'))
- g_norms_biases: float32 [6, 2048], P(None, ('dp', 'seq', 'tensor'))
Inputs may be any that keep to these rules, and one draw needn't show every extreme that they name: `lengths`: the number of real tokens at the start of each row; the rest of the row is padding.
All inputs are finite; a program needn't handle non-finite values.
Results may differ from a plain program's by a relative error of at most 0.012.
Values may be sent and summed in bfloat16 or wider, within the bound.
A program may use at most 256 MiB of HBM per device.

v0:
```python
import math
import jax
import jax.numpy as jnp
from jax import lax
from jax.sharding import PartitionSpec as P

NORM_EPS = 1e-05


def normalize(values_in):
    row_mean = jnp.mean(values_in, -1, keepdims=True)
    centered = values_in - row_mean
    variance = jnp.mean(centered * centered, -1, keepdims=True)
    inv_std = lax.rsqrt(variance + NORM_EPS)
    return (centered * inv_std, inv_std)


def norm_back(grad_in, normed, inv_std, norm_gain):
    scaled = grad_in * norm_gain
    mean_scaled = jnp.mean(scaled, -1, keepdims=True)
    mean_mixed = jnp.mean(scaled * normed, -1, keepdims=True)
    return inv_std * (scaled - mean_scaled - normed * mean_mixed)


def across_rows(left_in, right_in):
    return lax.dot_general(
        left_in, right_in, (((0,), (0,)), ((), ())), preferred_element_type=jnp.float32
    )


def times_transposed(left_in, right_in):
    return lax.dot_general(
        left_in, right_in, (((1,), (1,)), ((), ())), preferred_element_type=jnp.float32
    )


def shards(
    layer_input,
    lengths,
    cotangent,
    ln1_gain,
    ln1_bias,
    w_query,
    b_query,
    w_kv,
    b_value,
    w_out,
    b_out,
    ln2_gain,
    ln2_bias,
    w_up,
    b_up,
    w_down,
    b_down,
):
    n_rows, seq_len, model_width = layer_input.shape
    share_len = seq_len // lax.axis_size("tensor")
    tensor_index = lax.axis_index("tensor")
    seq_index = lax.axis_index("seq")
    full_len = seq_len * lax.axis_size("seq")
    head_size = w_kv.shape[1] // 2
    num_heads = w_query.shape[1] // head_size
    q_scale = 1.0 / math.sqrt(head_size)

    def own_rows(values_in):
        return lax.dynamic_slice_in_dim(values_in, tensor_index * share_len, share_len, 1)

    positions = seq_index * seq_len + jnp.arange(seq_len, dtype=jnp.int32)
    key_places = jnp.arange(full_len, dtype=jnp.int32)
    is_valid = (positions[None, :] < lengths[:, None]).astype(jnp.float32)
    allowed_keys = (key_places[None, None, :] <= positions[None, :, None]) & (
        key_places[None, None, :] < lengths[:, None, None]
    )
    valid_own = own_rows(is_valid)
    x_float = layer_input.astype(jnp.float32)
    normed_x1, inv_one = normalize(x_float)
    normed_one = (normed_x1 * ln1_gain + ln1_bias).astype(jnp.bfloat16)
    flat_one = normed_one.reshape(n_rows * seq_len, model_width)
    queries = (
        (jnp.dot(flat_one, w_query, preferred_element_type=jnp.float32) + b_query) * q_scale
    ).astype(jnp.bfloat16)
    queries = queries.reshape(n_rows, seq_len, num_heads, head_size)
    kv_bias = jnp.concatenate([jnp.zeros((head_size,), jnp.float32), b_value.astype(jnp.float32)])
    kv_local = (jnp.dot(flat_one, w_kv, preferred_element_type=jnp.float32) + kv_bias).astype(
        jnp.bfloat16
    )
    kv_local = kv_local.reshape(n_rows, seq_len, 2 * head_size)
    kv_all = lax.all_gather(kv_local, "seq", axis=1, tiled=True)
    key_rows = kv_all[..., :head_size]
    value_rows = kv_all[..., head_size:]

    def scores_of(query_rows):
        raw_scores = jnp.einsum(
            "rshd,rld->rhsl", query_rows, key_rows, preferred_element_type=jnp.float32
        )
        return jnp.where(allowed_keys[:, None], raw_scores, -1e30)

    scores = scores_of(queries)
    row_max = jnp.max(scores, -1, keepdims=True)
    exp_scores = jnp.exp(scores - row_max)
    exp_total = jnp.sum(exp_scores, -1, keepdims=True)
    soft_probs = exp_scores / exp_total
    log_total = row_max + jnp.log(exp_total)
    mixed_heads = jnp.einsum(
        "rhsl,rld->rshd",
        soft_probs.astype(jnp.bfloat16),
        value_rows,
        preferred_element_type=jnp.float32,
    ).astype(jnp.bfloat16)
    mixed_heads = mixed_heads.reshape(n_rows * seq_len, num_heads * head_size)
    attn_part = jnp.dot(mixed_heads, w_out, preferred_element_type=jnp.float32).reshape(
        n_rows, seq_len, model_width
    )
    residual = x_float + (lax.psum(attn_part, "tensor") + b_out)
    normed_x2, inv_two = normalize(residual)
    normed_two = (normed_x2 * ln2_gain + ln2_bias).astype(jnp.bfloat16)
    resid_own = own_rows(residual)
    normed_x2_own = own_rows(normed_x2)
    flat_two = normed_two.reshape(n_rows * seq_len, model_width)
    pre_act = jnp.dot(flat_two, w_up, preferred_element_type=jnp.float32) + b_up
    activated, gelu_pull = jax.vjp(
        lambda inner_in: jax.nn.gelu(inner_in, approximate=True), pre_act
    )
    act_low = activated.astype(jnp.bfloat16)
    mlp_part = jnp.dot(act_low, w_down, preferred_element_type=jnp.float32).reshape(
        n_rows, seq_len, model_width
    )
    mlp_own = (
        lax.psum_scatter(
            mlp_part.astype(jnp.bfloat16), "tensor", scatter_dimension=1, tiled=True
        ).astype(jnp.float32)
        + b_down
    )
    y_own = (valid_own[..., None] * (resid_own + mlp_own)).astype(jnp.bfloat16)
    cot_full = lax.all_gather(cotangent, "tensor", axis=1, tiled=True)
    grad_y = cot_full.astype(jnp.float32) * is_valid[..., None]
    grad_y_low = grad_y.astype(jnp.bfloat16).reshape(n_rows * seq_len, model_width)
    grad_y_own = cotangent.astype(jnp.float32) * valid_own[..., None]
    g_w_down = across_rows(act_low, grad_y_low)
    grad_act = times_transposed(grad_y_low, w_down)
    grad_pre = gelu_pull(grad_act)[0].astype(jnp.bfloat16)
    g_w_up = across_rows(flat_two, grad_pre)
    g_b_up = jnp.sum(grad_pre.astype(jnp.float32), axis=0)
    grad_a2 = times_transposed(grad_pre, w_up).reshape(n_rows, seq_len, model_width)
    grad_n2 = lax.psum(grad_a2, "tensor")
    grad_resid = grad_y + norm_back(grad_n2, normed_x2, inv_two, ln2_gain)
    grad_resid_low = grad_resid.astype(jnp.bfloat16)
    grad_resid_own = own_rows(grad_resid)
    grad_n2_own = own_rows(grad_n2)
    grad_resid_own_low = own_rows(grad_resid_low)
    g_ln2_gain = jnp.sum(grad_n2_own * normed_x2_own, axis=(0, 1))
    g_ln2_bias = jnp.sum(grad_n2_own, axis=(0, 1))
    g_b_out = jnp.sum(grad_resid_own_low.astype(jnp.float32), axis=(0, 1))
    g_b_down = jnp.sum(grad_y_own, axis=(0, 1))
    flat_resid = grad_resid_low.reshape(n_rows * seq_len, model_width)
    g_w_out = across_rows(mixed_heads, flat_resid)
    grad_mixed = times_transposed(flat_resid, w_out).astype(jnp.bfloat16)
    grad_mixed = grad_mixed.reshape(n_rows, seq_len, num_heads, head_size)
    again_probs = jnp.exp(scores_of(queries) - log_total)
    grad_probs = jnp.einsum(
        "rshd,rld->rhsl", grad_mixed, value_rows, preferred_element_type=jnp.float32
    )
    inner_sum = jnp.sum(again_probs * grad_probs, -1, keepdims=True)
    grad_scores = (again_probs * (grad_probs - inner_sum)).astype(jnp.bfloat16)
    grad_query = jnp.einsum(
        "rhsl,rld->rshd", grad_scores, key_rows, preferred_element_type=jnp.float32
    ).astype(jnp.bfloat16)
    grad_keys = jnp.einsum(
        "rhsl,rshd->rld", grad_scores, queries, preferred_element_type=jnp.float32
    )
    grad_values = jnp.einsum(
        "rhsl,rshd->rld",
        again_probs.astype(jnp.bfloat16),
        grad_mixed,
        preferred_element_type=jnp.float32,
    )
    grad_kv = jnp.concatenate([grad_keys, grad_values], -1)
    grad_kv_own = lax.psum_scatter(
        grad_kv, ("seq", "tensor"), scatter_dimension=1, tiled=True
    ).astype(jnp.bfloat16)
    flat_query = grad_query.reshape(n_rows * seq_len, num_heads * head_size)
    g_w_query = across_rows(flat_one, flat_query) * q_scale
    g_b_query = jnp.sum(flat_query.astype(jnp.float32), axis=0) * q_scale
    grad_n1_part = (times_transposed(flat_query, w_query) * q_scale).reshape(
        n_rows, seq_len, model_width
    )
    grad_n1_own = lax.psum_scatter(
        grad_n1_part.astype(jnp.bfloat16), "tensor", scatter_dimension=1, tiled=True
    ).astype(jnp.float32)
    flat_kv = grad_kv_own.reshape(n_rows * share_len, 2 * head_size)
    grad_n1_own = grad_n1_own + times_transposed(flat_kv, w_kv).reshape(
        n_rows, share_len, model_width
    )
    one_own = own_rows(normed_one).reshape(n_rows * share_len, model_width)
    g_w_kv = across_rows(one_own, flat_kv)
    g_b_value = jnp.sum(flat_kv[:, head_size:].astype(jnp.float32), axis=0)
    normed_x1_own = own_rows(normed_x1)
    x_grad_own = grad_resid_own + norm_back(grad_n1_own, normed_x1_own, own_rows(inv_one), ln1_gain)
    g_ln1_gain = jnp.sum(grad_n1_own * normed_x1_own, axis=(0, 1))
    g_ln1_bias = jnp.sum(grad_n1_own, axis=(0, 1))
    query_table = g_b_query.reshape(num_heads, head_size)
    up_table = g_b_up.reshape(-1, 128)
    summed = (
        lax.psum_scatter(g_w_query, ("dp", "seq"), scatter_dimension=0, tiled=True),
        lax.psum_scatter(query_table, ("dp", "seq"), scatter_dimension=1, tiled=True),
        lax.psum_scatter(g_w_out, ("dp", "seq"), scatter_dimension=1, tiled=True),
        lax.psum_scatter(g_w_up, ("dp", "seq"), scatter_dimension=0, tiled=True),
        lax.psum_scatter(up_table, ("dp", "seq"), scatter_dimension=1, tiled=True),
        lax.psum_scatter(g_w_down, ("dp", "seq"), scatter_dimension=1, tiled=True),
    )
    small_grads = jnp.stack([g_ln1_gain, g_ln1_bias, g_ln2_gain, g_ln2_bias, g_b_out, g_b_down])
    shared = (
        lax.psum_scatter(g_w_kv, ("dp", "seq", "tensor"), scatter_dimension=0, tiled=True),
        lax.psum_scatter(small_grads, ("dp", "seq", "tensor"), scatter_dimension=1, tiled=True),
        lax.psum_scatter(g_b_value, ("dp", "seq", "tensor"), scatter_dimension=0, tiled=True),
    )
    return (
        y_own,
        x_grad_own,
        summed[0],
        summed[1],
        shared[0],
        shared[2],
        summed[2],
        summed[3],
        summed[4],
        summed[5],
        shared[1],
    )


def solution(mesh):
    placed = (
        P("dp", "seq", None),
        P("dp"),
        P("dp", ("seq", "tensor"), None),
        P(),
        P(),
        P(None, "tensor"),
        P("tensor"),
        P(),
        P(),
        P("tensor", None),
        P(),
        P(),
        P(),
        P(None, "tensor"),
        P("tensor"),
        P("tensor", None),
        P(),
    )
    return jax.shard_map(
        shards,
        mesh=mesh,
        in_specs=placed,
        out_specs=(
            P("dp", ("seq", "tensor"), None),
            P("dp", ("seq", "tensor"), None),
            P(("dp", "seq"), "tensor"),
            P("tensor", ("dp", "seq")),
            P(("dp", "seq", "tensor"), None),
            P(("dp", "seq", "tensor")),
            P("tensor", ("dp", "seq")),
            P(("dp", "seq"), "tensor"),
            P("tensor", ("dp", "seq")),
            P("tensor", ("dp", "seq")),
            P(None, ("dp", "seq", "tensor")),
        ),
        check_vma=False,
    )
```

profile of v0, /device:TPU:0, one launch (start us, length us, event | category | flops | bytes accessed | tf_op | source)
XLA Modules:
  0.0 1648.8 jit_solution(9399819819224728491)
XLA Ops:
  8.1 2.6 convert_reduce_fusion
  10.7 2.9 fusion.8
  13.7 3.3 fusion.6
  21.5 5.2 multiply_convert_fusion.3
  30.5 29.8 %all-gather.3.cloned.1.call-done = bf16[3,1024,256]{2,1,0:T(8,128)(2,1)} async-done(((bf16[3,256,256]{2,1,0:T(8,128)(2,1)}), bf16[3,1024,256]{2,1,0:T(8,128)(2,1)}) %all-gather.3.cloned.1.call-update) | async-done | bytes 1572880 | tf_op jit(solution)/shard_map/all_gather | solution.py:88
  60.4 7.9 fusion.4
  68.3 7.4 fusion.3
  75.8 6.5 fusion.28
  83.2 4.4 fusion.23
  89.3 4.1 fusion.19
  93.4 117.9 %all-reduce.7.cloned.1.call-done = f32[3,256,2048]{2,1,0:T(8,128)} async-done(((f32[3,256,2048]{2,1,0:T(8,128)}), f32[3,256,2048]{2,1,0:T(8,128)}) %all-reduce.7.cloned.1.call-update) | async-done | bytes 6291472 | tf_op jit(solution)/shard_map/psum | solution.py:114
  211.3 4.6 fusion.48
  216.8 4.1 add_convert_fusion
  222.1 2.8 slice-done.1
  224.9 8.5 fusion.49
  233.4 14.9 convert_reduce_fusion.1
  248.3 8.6 fusion.50
  257.0 13.3 convolution_convert_fusion
  270.3 106.6 %all-reduce.9.cloned.1.call-done = f32[3,256,2048]{2,1,0:T(8,128)} async-done(((f32[3,256,2048]{2,1,0:T(8,128)}), f32[3,256,2048]{2,1,0:T(8,128)}) %all-reduce.9.cloned.1.call-update) | async-done | bytes 6291472 | tf_op jit(solution)/shard_map/psum | solution.py:145
  376.9 5.9 multiply_reduce_fusion.2
  384.2 6.1 fusion.47
  391.9 2.8 convolution_convert_fusion.1
  394.7 2.4 reshape.237
  399.3 8.6 fusion
  407.9 6.7 fusion.2
  414.7 2.7 copy-done.2
  419.4 2.2 copy.64
  421.6 5.3 multiply_convert_fusion
  429.4 9.6 fusion.25
  439.0 6.1 convolution_bitcast_fusion.1
  445.8 4.0 pad_maximum_fusion
  449.8 5.0 copy.69
  454.8 98.2 %all-reduce.10 = bf16[3,1024,256]{2,0,1:T(4,128)(2,1)} all-reduce(f32[3,1024,256]{2,0,1:T(4,128)} %copy.69), channel_id=4, replica_groups=mesh['dp'=2,'seq'=4,'tensor'=4] {'seq','tensor'}, use_global_device_ids=true, to_apply=%region_13.14.clone | all-reduce | flops 786432 | bytes 4718592
  557.5 3.0 multiply_reduce_fusion.3
  560.5 3.9 multiply_reduce_fusion.5
  565.8 3.0 convolution_bitcast_fusion
  570.2 6.0 fusion.32
  576.3 5.7 convolution_multiply_fusion
  582.3 13.9 fusion.45
  596.3 12.5 fusion.51
  611.0 40.6 %all-reduce.2 = f32[128]{0:T(128)S(1)} all-reduce(f32[128]{0:T(128)S(1)} %convert_reduce_fusion.4), channel_id=8, replica_groups=mesh['dp'=2,'seq'=4,'tensor'=4] {'dp','seq','tensor'}, use_global_device_ids=true, to_apply=%region_21.22.clone | all-reduce | flops 128 | bytes 1024
  653.6 3.9 multiply_add_fusion.1
  657.5 99.5 %reduce-scatter.35.cloned.1.call-done = f32[64,6]{1,0:T(8,128)} async-done(((f32[2048,6]{1,0:T(8,128)}), f32[64,6]{1,0:T(8,128)}) %reduce-scatter.35.cloned.1.call-update) | async-done | bytes 1552
  758.4 135.5 %reduce-scatter.23.cloned.1.call-done = f32[64,256]{1,0:T(8,128)} async-done(((f32[2048,256]{1,0:T(8,128)}), f32[64,256]{1,0:T(8,128)}) %reduce-scatter.23.cloned.1.call-update) | async-done | bytes 65552 | tf_op jit(solution)/shard_map/reduce_scatter | solution.py:213
  893.9 89.4 %reduce-scatter.25.cloned.1.call-done = f32[512,256]{1,0:T(8,128)} async-done(((f32[512,2048]{1,0:T(8,128)}), f32[512,256]{1,0:T(8,128)}) %reduce-scatter.25.cloned.1.call-update) | async-done | bytes 524304 | tf_op jit(solution)/shard_map/reduce_scatter | solution.py:206
  983.4 92.0 %reduce-scatter.21.cloned.1.call-done = f32[256,512]{1,0:T(8,128)} async-done(((f32[2048,512]{1,0:T(8,128)}), f32[256,512]{1,0:T(8,128)}) %reduce-scatter.21.cloned.1.call-update) | async-done | bytes 524304 | tf_op jit(solution)/shard_map/reduce_scatter | solution.py:204
  1075.4 283.5 %reduce-scatter.29.cloned.1.call-done = f32[2048,256]{1,0:T(8,128)} async-done(((f32[2048,2048]{1,0:T(8,128)}), f32[2048,256]{1,0:T(8,128)}) %reduce-scatter.29.cloned.1.call-update) | async-done | bytes 2097168 | tf_op jit(solution)/shard_map/reduce_scatter | solution.py:209
  1358.9 282.9 %reduce-scatter.27.cloned.1.call-done = f32[256,2048]{1,0:T(8,128)} async-done(((f32[2048,2048]{1,0:T(8,128)}), f32[256,2048]{1,0:T(8,128)}) %reduce-scatter.27.cloned.1.call-update) | async-done | bytes 2097168 | tf_op jit(solution)/shard_map/reduce_scatter | solution.py:207
  (148 shorter events, 36.8 us)
Async XLA Ops:
  7.2 76.0 %copy-start = (bf16[512,2048]{1,0:T(8,128)(2,1)S(1)}, bf16[512,2048]{1,0:T(8,128)(2,1)}, u32[]{:S(2)}) copy-start(bf16[512,2048]{1,0:T(8,128)(2,1)} %param.26) | copy-start | bytes 6291460
  7.2 6.4 copy-start.22
  7.2 6.4 copy-start.23
  7.2 53.2 %all-gather.3.cloned.1.call-start = ((), (), s32[]{:S(2)}) async-start(), calls=%async_computation.10 | async-start | bytes 1966080 | tf_op jit(solution)/shard_map/all_gather | solution.py:88
  7.3 6.4 copy-start.3
  13.6 3.4 copy-start.20
  13.6 3.4 copy-start.18
  13.7 5.0 copy-start.16
  17.0 1.7 copy-start.8
  17.0 4.5 copy-start.30
  20.5 68.9 %all-gather.5.cloned.1.call-start = ((), (), s32[]{:S(2)}) async-start(), calls=%async_computation.13 | async-start | bytes 3932160 | tf_op jit(solution)/shard_map/all_gather | solution.py:135
  21.2 190.1 %all-reduce.7.cloned.1.call-start = ((), (), s32[]{:S(2)}) async-start(), calls=%async_computation.11 | async-start | bytes 12582912 | tf_op jit(solution)/shard_map/psum | solution.py:114
  21.5 8.2 copy-start.29
  68.3 7.5 copy-start.9
  82.3 0.9 copy-start.11
  83.2 4.5 copy-start.24
  83.2 4.5 copy-start.25
  83.2 4.6 copy-start.26
  83.2 4.6 copy-start.27
  87.7 289.2 %all-reduce.9.cloned.1.call-start = ((), (), s32[]{:S(2)}) async-start(), calls=%async_computation.14 | async-start | bytes 12582912 | tf_op jit(solution)/shard_map/psum | solution.py:145
  215.9 6.2 copy-start.1
  216.0 6.2 slice-start
  216.7 8.2 slice-start.1
  222.1 11.3 copy-start.14
  224.9 8.5 copy-start.13
  248.3 8.6 copy-start.32
  256.9 300.6 %reduce-scatter.17.cloned.1.call-start = ((), (), s32[]{:S(2)}) async-start(), calls=%async_computation.12 | async-start | bytes 3932160 | tf_op jit(solution)/shard_map/reduce_scatter | solution.py:129
  270.2 290.2 %reduce-scatter.19.cloned.1.call-start = ((), (), s32[]{:S(2)}) async-start(), calls=%async_computation.15 | async-start | bytes 3932160 | tf_op jit(solution)/shard_map/reduce_scatter | solution.py:187
  376.9 6.4 copy-start.4
  376.9 7.3 copy-start.6
  390.3 1.6 copy-start.5
  407.9 9.5 copy-start.10
  414.7 2.8 copy-start.2
  421.6 5.4 copy-start.28
  421.6 5.4 copy-start.31
  426.9 182.6 %reduce-scatter.33.cloned.1.call-start = ((), (), s32[]{:S(2)}) async-start(), calls=%async_computation.22 | async-start | bytes 73728
  429.1 223.1 %reduce-scatter.31.cloned.1.call-start = ((), (), s32[]{:S(2)}) async-start(), calls=%async_computation.21 | async-start | bytes 73728
  429.4 9.6 copy-start.7
  454.8 102.7 %copy-start.15 = (bf16[3,64,2048]{2,1,0:T(8,128)(2,1)S(1)}, bf16[3,64,2048]{2,1,0:T(8,128)(2,1)}, u32[]{:S(2)}) copy-start(bf16[3,64,2048]{2,1,0:T(8,128)(2,1)} %param.19) | copy-start | bytes 2359300
  454.8 105.7 %copy-start.19 = (f32[2048]{0:T(1024)S(1)}, f32[2048]{0:T(1024)}, u32[]{:S(2)}) copy-start(f32[2048]{0:T(1024)} %copy-done.18) | copy-start | bytes 24580
  555.3 201.7 %reduce-scatter.35.cloned.1.call-start = ((), (), s32[]{:S(2)}) async-start(), calls=%async_computation.23 | async-start | bytes 1081344
  560.5 8.4 copy-start.12
  565.8 328.1 %reduce-scatter.23.cloned.1.call-start = ((), (), s32[]{:S(2)}) async-start(), calls=%async_computation.17 | async-start | bytes 2162688 | tf_op jit(solution)/shard_map/reduce_scatter | solution.py:213
  568.8 414.5 %reduce-scatter.25.cloned.1.call-start = ((), (), s32[]{:S(2)}) async-start(), calls=%async_computation.18 | async-start | bytes 4718592 | tf_op jit(solution)/shard_map/reduce_scatter | solution.py:206
  570.2 6.1 copy-start.17
  576.2 499.1 %reduce-scatter.21.cloned.1.call-start = ((), (), s32[]{:S(2)}) async-start(), calls=%async_computation.16 | async-start | bytes 4718592 | tf_op jit(solution)/shard_map/reduce_scatter | solution.py:204
  582.0 776.9 %reduce-scatter.29.cloned.1.call-start = ((), (), s32[]{:S(2)}) async-start(), calls=%async_computation.20 | async-start | bytes 18874368 | tf_op jit(solution)/shard_map/reduce_scatter | solution.py:209
  596.2 1045.5 %reduce-scatter.27.cloned.1.call-start = ((), (), s32[]{:S(2)}) async-start(), calls=%async_computation.19 | async-start | bytes 18874368 | tf_op jit(solution)/shard_map/reduce_scatter | solution.py:207
  (1 other events, 0.7 us)
Sparse Core Ops, SparseCore 0:
  20.6 39.7 all-gather.2
  61.9 27.3 all-gather.4
  91.7 119.5 all-reduce.6
  257.0 119.7 all-reduce.8
  379.2 37.9 reduce-scatter.16
  427.1 42.3 reduce-scatter.18
  472.9 66.0 reduce-scatter.32
  555.4 63.4 reduce-scatter.30
  621.2 135.7 reduce-scatter.34
  759.7 134.2 reduce-scatter.22
  898.2 85.1 reduce-scatter.24
  987.4 87.9 reduce-scatter.20
  1079.7 279.1 reduce-scatter.28
  1363.1 278.6 reduce-scatter.26
where the time goes:
time: 1650 us
  waiting for transfers between devices  1240 us (75%)
  matrix products  150 us (9%)
  blocking collectives  139 us (8%)
  other arithmetic  64.6 us (4%)
  local copies, waits for them, and re-layouts  38.7 us (2%)
    reduce_scatter x1, waiting for transfers between devices, shards(): lax.psum_scatter(g_w_down, ('dp', 'seq'), scatter_dimension=1, tiled=True)  284 us
    reduce_scatter x1, waiting for transfers between devices, shards(): lax.psum_scatter(g_w_up, ('dp', 'seq'), scatter_dimension=0, tiled=True)  283 us
    unnamed x2, blocking collectives  139 us
    reduce_scatter x1, waiting for transfers between devices, shards(): lax.psum_scatter(g_w_kv, ('dp', 'seq', 'tensor'), scatter_dimension=0, ti...  136 us
    psum x1, waiting for transfers between devices, shards(): residual = x_float + (lax.psum(attn_part, 'tensor') + b_out)  118 us
    psum x1, waiting for transfers between devices, shards(): grad_n2 = lax.psum(grad_a2, 'tensor')  107 us
    unnamed x17, waiting for transfers between devices  100 us
    reduce_scatter x1, waiting for transfers between devices, shards(): lax.psum_scatter(g_w_query, ('dp', 'seq'), scatter_dimension=0, tiled=True)  92 us
  transfers between devices with their start and end apart: 14, of which 10 were waited for; matrix products, arithmetic and copies ran while one was open for 11% of the time, Pallas kernels for 0%

commit v1 on v0

--- a/solution.py
+++ b/solution.py
@@ -3,6 +3,7 @@
 import jax.numpy as jnp
 from jax import lax
 from jax.sharding import PartitionSpec as P
+from jax.lax import axis_size, ppermute
 
 NORM_EPS = 1e-05
 
@@ -142,7 +143,12 @@
     g_w_up = across_rows(flat_two, grad_pre)
     g_b_up = jnp.sum(grad_pre.astype(jnp.float32), axis=0)
     grad_a2 = times_transposed(grad_pre, w_up).reshape(n_rows, seq_len, model_width)
-    grad_n2 = lax.psum(grad_a2, "tensor")
+    how_many = axis_size("tensor")
+    grad_n2 = grad_a2
+    for dev in [j for j in (1, 2, 4, 8, 16) if j < how_many]:
+        grad_n2 = grad_n2 + ppermute(
+            grad_n2, axis_name="tensor", perm=tuple(((m, m ^ dev) for m in range(how_many)))
+        )
     grad_resid = grad_y + norm_back(grad_n2, normed_x2, inv_two, ln2_gain)
     grad_resid_low = grad_resid.astype(jnp.bfloat16)
     grad_resid_own = own_rows(grad_resid)

time: 1650 us -> 1710 us (1.036)
  waiting for transfers between devices: 1240 us -> 1290 us
    ppermute x0 -> x2, waiting for transfers between devices: none -> 151 us  [shards(): ppermute(grad_n2, axis_name='tensor', perm=tuple(((m, m ^ dev) for m in r...]
    psum x1 -> x0, waiting for transfers between devices: 107 us -> none  [shards(): grad_n2 = lax.psum(grad_a2, 'tensor')]
    unnamed x17 -> x16, waiting for transfers between devices: 100 us -> 104 us
  transfers between devices with their start and end apart: 14 -> 15, of which waited for: 10 -> 11; matrix products, arithmetic and copies ran while one was open for 11% -> 11% of each run, Pallas kernels for 0% -> 0%
where the time goes in v1:
time: 1710 us; the launch traced here: 1700 us
  waiting for transfers between devices  1290 us (75%)
  matrix products  148 us (9%)
  blocking collectives  137 us (8%)
  other arithmetic  75.6 us (4%)
  local copies, waits for them, and re-layouts  37.7 us (2%)
    reduce_scatter x1, waiting for transfers between devices, shards(): lax.psum_scatter(g_w_down, ('dp', 'seq'), scatter_dimension=1, tiled=True)  283 us
    reduce_scatter x1, waiting for transfers between devices, shards(): lax.psum_scatter(g_w_up, ('dp', 'seq'), scatter_dimension=0, tiled=True)  283 us
    ppermute x2, waiting for transfers between devices, shards(): ppermute(grad_n2, axis_name='tensor', perm=tuple(((m, m ^ dev) for m in r...  151 us
    unnamed x2, blocking collectives  137 us
    reduce_scatter x1, waiting for transfers between devices, shards(): lax.psum_scatter(g_w_kv, ('dp', 'seq', 'tensor'), scatter_dimension=0, ti...  136 us
    psum x1, waiting for transfers between devices, shards(): residual = x_float + (lax.psum(attn_part, 'tensor') + b_out)  118 us
    unnamed x16, waiting for transfers between devices  104 us
    reduce_scatter x1, waiting for transfers between devices, shards(): lax.psum_scatter(g_w_query, ('dp', 'seq'), scatter_dimension=0, tiled=True)  92.2 us
  transfers between devices with their start and end apart: 15, of which 11 were waited for; matrix products, arithmetic and copies ran while one was open for 11% of the time, Pallas kernels for 0%

profile of v1, /device:TPU:0, one launch (start us, length us, event | category | flops | bytes accessed | tf_op | source)
XLA Modules:
  0.0 1703.6 jit_solution(18213577887150798395)
XLA Ops:
  8.1 2.6 convert_reduce_fusion
  10.7 2.9 fusion.8
  13.7 3.3 fusion.6
  21.6 5.2 multiply_convert_fusion.3
  30.6 29.8 %all-gather.3.cloned.1.call-done = bf16[3,1024,256]{2,1,0:T(8,128)(2,1)} async-done(((bf16[3,256,256]{2,1,0:T(8,128)(2,1)}), bf16[3,1024,256]{2,1,0:T(8,128)(2,1)}) %all-gather.3.cloned.1.call-update) | async-done | bytes 1572880 | tf_op jit(solution)/shard_map/all_gather | solution.py:89
  60.4 7.9 fusion.4
  68.3 7.4 fusion.3
  75.8 6.5 fusion.28
  83.2 4.5 fusion.23
  89.3 4.1 fusion.19
  93.4 117.9 %all-reduce.6.cloned.1.call-done = f32[3,256,2048]{2,1,0:T(8,128)} async-done(((f32[3,256,2048]{2,1,0:T(8,128)}), f32[3,256,2048]{2,1,0:T(8,128)}) %all-reduce.6.cloned.1.call-update) | async-done | bytes 6291472 | tf_op jit(solution)/shard_map/psum | solution.py:115
  211.3 4.6 fusion.48
  216.7 3.7 add_convert_fusion
  222.1 2.8 slice-done.3
  224.9 6.7 fusion.49
  231.7 16.3 convert_reduce_fusion.1
  248.0 8.6 fusion.50
  256.7 10.1 collective-permute-done
  266.8 3.9 add.189
  271.3 13.1 convolution_convert_fusion
  284.5 141.0 %collective-permute-done.1 = f32[3,256,2048]{2,1,0:T(8,128)} collective-permute-done((f32[3,256,2048]{2,1,0:T(8,128)}, f32[3,256,2048]{2,1,0:T(8,128)}, u32[]{:S(2)}, u32[]{:S(2)}) %collective-permute-start.1) | collective-permute-done | bytes 6291488 | tf_op jit(solution)/shard_map/ppermute | solution.py:149
  425.5 9.9 multiply_reduce_fusion.2
  435.4 9.0 fusion.47
  446.2 2.8 convolution_convert_fusion.1
  453.6 8.6 fusion
  462.2 6.6 fusion.2
  468.8 2.7 copy-done.2
  475.7 5.4 multiply_convert_fusion
  483.8 3.3 multiply_reduce_fusion.3
  489.5 9.7 fusion.25
  499.3 3.3 convolution_bitcast_fusion.1
  503.3 3.9 pad_maximum_fusion
  507.2 5.0 copy.69
  512.2 95.3 %all-reduce.7 = bf16[3,1024,256]{2,0,1:T(4,128)(2,1)} all-reduce(f32[3,1024,256]{2,0,1:T(4,128)} %copy.69), channel_id=4, replica_groups=mesh['dp'=2,'seq'=4,'tensor'=4] {'seq','tensor'}, use_global_device_ids=true, to_apply=%region_12.13.clone | all-reduce | flops 786432 | bytes 4718592
  609.8 3.9 multiply_reduce_fusion.5
  615.2 3.0 convolution_bitcast_fusion
  619.6 6.0 fusion.32
  625.6 5.7 convolution_multiply_fusion
  631.6 14.0 fusion.45
  645.7 12.8 fusion.51
  660.7 41.7 %all-reduce.2 = f32[128]{0:T(128)S(1)} all-reduce(f32[128]{0:T(128)S(1)} %convert_reduce_fusion.4), channel_id=8, replica_groups=mesh['dp'=2,'seq'=4,'tensor'=4] {'dp','seq','tensor'}, use_global_device_ids=true, to_apply=%region_20.21.clone | all-reduce | flops 128 | bytes 1024
  704.4 3.9 multiply_add_fusion.1
  708.3 103.4 %reduce-scatter.35.cloned.1.call-done = f32[64,6]{1,0:T(8,128)} async-done(((f32[2048,6]{1,0:T(8,128)}), f32[64,6]{1,0:T(8,128)}) %reduce-scatter.35.cloned.1.call-update) | async-done | bytes 1552
  813.2 136.2 %reduce-scatter.23.cloned.1.call-done = f32[64,256]{1,0:T(8,128)} async-done(((f32[2048,256]{1,0:T(8,128)}), f32[64,256]{1,0:T(8,128)}) %reduce-scatter.23.cloned.1.call-update) | async-done | bytes 65552 | tf_op jit(solution)/shard_map/reduce_scatter | solution.py:219
  949.4 89.0 %reduce-scatter.25.cloned.1.call-done = f32[512,256]{1,0:T(8,128)} async-done(((f32[512,2048]{1,0:T(8,128)}), f32[512,256]{1,0:T(8,128)}) %reduce-scatter.25.cloned.1.call-update) | async-done | bytes 524304 | tf_op jit(solution)/shard_map/reduce_scatter | solution.py:212
  1038.3 92.2 %reduce-scatter.21.cloned.1.call-done = f32[256,512]{1,0:T(8,128)} async-done(((f32[2048,512]{1,0:T(8,128)}), f32[256,512]{1,0:T(8,128)}) %reduce-scatter.21.cloned.1.call-update) | async-done | bytes 524304 | tf_op jit(solution)/shard_map/reduce_scatter | solution.py:210
  1130.5 283.4 %reduce-scatter.29.cloned.1.call-done = f32[2048,256]{1,0:T(8,128)} async-done(((f32[2048,2048]{1,0:T(8,128)}), f32[2048,256]{1,0:T(8,128)}) %reduce-scatter.29.cloned.1.call-update) | async-done | bytes 2097168 | tf_op jit(solution)/shard_map/reduce_scatter | solution.py:215
  1413.8 283.1 %reduce-scatter.27.cloned.1.call-done = f32[256,2048]{1,0:T(8,128)} async-done(((f32[2048,2048]{1,0:T(8,128)}), f32[256,2048]{1,0:T(8,128)}) %reduce-scatter.27.cloned.1.call-update) | async-done | bytes 2097168 | tf_op jit(solution)/shard_map/reduce_scatter | solution.py:213
  (151 shorter events, 41.6 us)
Async XLA Ops:
  7.2 76.0 %copy-start = (bf16[512,2048]{1,0:T(8,128)(2,1)S(1)}, bf16[512,2048]{1,0:T(8,128)(2,1)}, u32[]{:S(2)}) copy-start(bf16[512,2048]{1,0:T(8,128)(2,1)} %param.26) | copy-start | bytes 6291460
  7.2 6.4 copy-start.20
  7.2 6.4 copy-start.21
  7.2 53.2 %all-gather.3.cloned.1.call-start = ((), (), s32[]{:S(2)}) async-start(), calls=%async_computation.10 | async-start | bytes 1966080 | tf_op jit(solution)/shard_map/all_gather | solution.py:89
  7.3 6.4 copy-start.3
  13.6 3.4 copy-start.18
  13.6 3.4 copy-start.16
  13.7 5.0 copy-start.14
  17.0 1.7 copy-start.6
  17.0 4.6 copy-start.28
  20.5 68.9 %all-gather.5.cloned.1.call-start = ((), (), s32[]{:S(2)}) async-start(), calls=%async_computation.13 | async-start | bytes 3932160 | tf_op jit(solution)/shard_map/all_gather | solution.py:136
  21.2 190.1 %all-reduce.6.cloned.1.call-start = ((), (), s32[]{:S(2)}) async-start(), calls=%async_computation.11 | async-start | bytes 12582912 | tf_op jit(solution)/shard_map/psum | solution.py:115
  21.6 8.2 copy-start.27
  68.3 7.5 copy-start.7
  83.2 5.1 copy-start.22
  83.2 5.1 copy-start.23
  83.2 5.1 copy-start.24
  83.2 5.2 copy-start.25
  87.7 396.1 %reduce-scatter.17.cloned.1.call-start = ((), (), s32[]{:S(2)}) async-start(), calls=%async_computation.12 | async-start | bytes 3932160 | tf_op jit(solution)/shard_map/reduce_scatter | solution.py:130
  215.9 6.2 copy-start.1
  215.9 6.2 slice-start.2
  216.7 8.2 slice-start.3
  222.1 9.5 copy-start.13
  224.9 6.8 copy-start.12
  231.7 16.4 copy-start.30
  256.6 10.2 collective-permute-start
  270.8 154.7 %collective-permute-start.1 = (f32[3,256,2048]{2,1,0:T(8,128)}, f32[3,256,2048]{2,1,0:T(8,128)}, u32[]{:S(2)}, u32[]{:S(2)}) collective-permute-start(f32[3,256,2048]{2,1,0:T(8,128)} %add.189), channel_id=1, source_target_pairs={{0,2},{1,3},{2,0},{3,1},{4,6},{5,7},{6,4},{7,5},{8,10},{9,11},{10,... | collective-permute-start | bytes 18874376 | tf_op jit(solution)/shard_map/ppermute | solution.py:149
  284.4 325.4 %reduce-scatter.19.cloned.1.call-start = ((), (), s32[]{:S(2)}) async-start(), calls=%async_computation.14 | async-start | bytes 3932160 | tf_op jit(solution)/shard_map/reduce_scatter | solution.py:193
  444.4 1.8 copy-start.4
  462.2 9.4 copy-start.8
  468.8 2.7 copy-start.2
  475.7 5.5 copy-start.26
  475.7 5.5 copy-start.29
  481.1 178.2 %reduce-scatter.33.cloned.1.call-start = ((), (), s32[]{:S(2)}) async-start(), calls=%async_computation.21 | async-start | bytes 73728
  483.3 219.8 %reduce-scatter.31.cloned.1.call-start = ((), (), s32[]{:S(2)}) async-start(), calls=%async_computation.20 | async-start | bytes 73728
  483.8 5.7 copy-start.9
  487.1 12.2 slice-start
  489.5 9.7 slice-start.1
  489.5 9.7 copy-start.5
  507.2 102.6 %copy-start.17 = (f32[2048]{0:T(1024)S(1)}, f32[2048]{0:T(1024)}, u32[]{:S(2)}) copy-start(f32[2048]{0:T(1024)} %copy-done.16) | copy-start | bytes 24580
  609.7 8.5 copy-start.11
  609.7 202.0 %reduce-scatter.35.cloned.1.call-start = ((), (), s32[]{:S(2)}) async-start(), calls=%async_computation.22 | async-start | bytes 1081344
  615.1 334.2 %reduce-scatter.23.cloned.1.call-start = ((), (), s32[]{:S(2)}) async-start(), calls=%async_computation.16 | async-start | bytes 2162688 | tf_op jit(solution)/shard_map/reduce_scatter | solution.py:219
  618.2 420.2 %reduce-scatter.25.cloned.1.call-start = ((), (), s32[]{:S(2)}) async-start(), calls=%async_computation.17 | async-start | bytes 4718592 | tf_op jit(solution)/shard_map/reduce_scatter | solution.py:212
  619.6 6.1 copy-start.15
  625.6 504.9 %reduce-scatter.21.cloned.1.call-start = ((), (), s32[]{:S(2)}) async-start(), calls=%async_computation.15 | async-start | bytes 4718592 | tf_op jit(solution)/shard_map/reduce_scatter | solution.py:210
  631.4 782.4 %reduce-scatter.29.cloned.1.call-start = ((), (), s32[]{:S(2)}) async-start(), calls=%async_computation.19 | async-start | bytes 18874368 | tf_op jit(solution)/shard_map/reduce_scatter | solution.py:215
  645.7 1051.2 %reduce-scatter.27.cloned.1.call-start = ((), (), s32[]{:S(2)}) async-start(), calls=%async_computation.18 | async-start | bytes 18874368 | tf_op jit(solution)/shard_map/reduce_scatter | solution.py:213
  (2 other events, 1.6 us)
Sparse Core Ops, SparseCore 0:
  20.6 39.7 all-gather.2
  61.9 27.3 all-gather.4
  91.7 119.5 all-reduce.5
  284.5 55.6 reduce-scatter.16
  481.2 37.9 reduce-scatter.18
  522.5 62.5 reduce-scatter.32
  609.8 63.9 reduce-scatter.30
  676.1 135.6 reduce-scatter.34
  814.6 134.7 reduce-scatter.22
  953.4 84.8 reduce-scatter.24
  1042.5 87.9 reduce-scatter.20
  1134.7 279.1 reduce-scatter.28
  1418.2 278.6 reduce-scatter.26
